TPU v7x, 32 devices: a whole 2x2x4 slice. The times are simulated.
32 devices in a mesh: dp: 8 (over z, core), tp: 4 (over y, x).
Axes of the slice: x: 2, y: 2, z: 4, core: 2. Of those that a mesh axis runs over, the one named last changes fastest.
Arguments:
- x_in: bfloat16 [8192, 2048], P(('dp', 'tp')), may hold values from -6 to 6
- norm_gain: float32 [2048], replicated, may hold values from 0.5 to 1.5
- w_z: bfloat16 [2048, 4096], P(None, 'tp'), may hold values from -0.125 to 0.125
- w_x: bfloat16 [2048, 4096], P(None, 'tp'), may hold values from -0.125 to 0.125
- w_b: bfloat16 [2048, 128], P(None, 'tp'), may hold values from -0.125 to 0.125
- w_c: bfloat16 [2048, 128], P(None, 'tp'), may hold values from -0.125 to 0.125
- w_dt: bfloat16 [2048, 64], P(None, 'tp'), may hold values from -0.125 to 0.125
- conv_w: float32 [4352, 4], replicated, may hold values from -3 to 3
- conv_b: float32 [4352], replicated, may hold values from -3 to 3
- dt_bias: float32 [64], replicated, may hold values from -6 to -2
- a_log: float32 [64], replicated, may hold values from -2.5 to 0.5
- d_skip: float32 [64], replicated, may hold values from 0.5 to 1.5
- gate_gain: float32 [4096], replicated, may hold values from 0.5 to 1.5
- w_out: bfloat16 [4096, 2048], P('tp'), may hold values from -0.09375 to 0.09375
- doc_lens: int32 [8, 8], P('dp'), may hold values from 1 to 512, 1024 in all within a row
- d_out: bfloat16 [8192, 2048], P(('dp', 'tp')), may hold values from -6 to 6
Outputs:
- block_out: bfloat16 [8192, 2048], P(('dp', 'tp'))
- grad_x: float32 [8192, 2048], P(('dp', 'tp'))
- grad_norm_gain: float32 [2048], replicated
- grad_w_z: float32 [2048, 4096], P('dp', 'tp')
- grad_w_x: float32 [2048, 4096], P('dp', 'tp')
- grad_w_b: float32 [2048, 128], P('dp', 'tp')
- grad_w_c: float32 [2048, 128], P('dp', 'tp')
- grad_w_dt: float32 [2048, 64], P('dp', 'tp')
- grad_conv_w: float32 [4352, 4], replicated
- grad_conv_b: float32 [4352], replicated
- grad_dt_bias: float32 [64], replicated
- grad_a_log: float32 [64], replicated
- grad_d_skip: float32 [64], replicated
- grad_gate_gain: float32 [4096], replicated
- grad_w_out: float32 [4096, 2048], P('tp', 'dp')
Inputs may be any that keep to these rules, and one draw needn't show every extreme that they name: `doc_lens`: each row gives, in order, the lengths of the 8 documents packed into one sequence of 1024 tokens; a row sums to 1024 and its longest document has exactly 512 tokens.
All inputs are finite; a program needn't handle non-finite values.
Results may differ from a plain program's by a relative error of at most 0.012.
Values may be sent and summed in bfloat16 or wider, within the bound.
A program may use at most 256 MiB of HBM per device.

v0:
```python
import jax
import jax.numpy as jnp
from jax import lax
from jax.sharding import PartitionSpec as P

EPSILON = 1e-05
HIGHEST = lax.Precision.HIGHEST


def entering_2(array, axis, combine, identity, reverse):
    count, index = (lax.axis_size(axis), lax.axis_index(axis))
    everything = jax.tree.map(lambda part: lax.all_gather(part, axis), array)
    start = jax.tree.map(
        lambda part, zero: jnp.broadcast_to(jnp.asarray(zero, part.dtype), part.shape),
        array,
        identity,
    )

    def lap(k, before):
        at = count - 1 - k if reverse else k
        reached = at > index if reverse else at < index
        new = combine(before, jax.tree.map(lambda part: part[at], everything))
        return jax.tree.map(lambda a, b: jnp.where(reached, a, b), new, before)

    return lax.fori_loop(0, count, lap, start)


def span_parts(log_decay, segments, segment_prev):
    cumulative = jnp.cumsum(log_decay, axis=0)
    inward = jnp.exp(cumulative) * (segments == segment_prev).astype(jnp.float32)[:, None]
    carried = jnp.exp(cumulative[-1]) * (segments[-1] == segment_prev).astype(jnp.float32)
    return (cumulative, inward, carried)


def span_pass(state, values, b_rows, c_rows, log_decay, steps_dt, segments, segment_prev):
    cumulative, inward, carried = span_parts(log_decay, segments, segment_prev)
    length = segments.shape[0]
    order = jnp.arange(length, dtype=jnp.int32)
    same = (segments[:, None] == segments[None, :]) & (order[:, None] >= order[None, :])
    spread = cumulative[:, None, :] - cumulative[None, :, :]
    decays = jnp.exp(jnp.where(same[:, :, None], spread, -1e30))
    scores = jnp.dot(c_rows, b_rows.T, precision=HIGHEST)
    mixing = decays * scores[:, :, None] * steps_dt[None, :, :]
    output = jnp.einsum("tsh,shp->thp", mixing, values, precision=HIGHEST)
    output = (
        output + jnp.einsum("tn,hpn->thp", c_rows, state, precision=HIGHEST) * inward[:, :, None]
    )
    tail_same = segments == segments[-1]
    tail = (
        jnp.exp(jnp.where(tail_same[:, None], cumulative[-1][None, :] - cumulative, -1e30))
        * steps_dt
    )
    weighted = tail[:, :, None] * values
    state_out = carried[:, None, None] * state + jnp.einsum(
        "shp,sn->hpn", weighted, b_rows, precision=HIGHEST
    )
    return (output, state_out, carried)


def in_norm(values, gain):
    return (
        values
        * lax.rsqrt(jnp.mean(values * values, axis=-1, keepdims=True) + EPSILON)
        * gain[None, :]
    )


def combine(earlier, later):
    return (earlier[0] * later[0], later[0][:, None, None] * earlier[1] + later[1])


def body(
    x_in,
    norm_gain,
    w_z,
    w_x,
    w_b,
    w_c,
    w_dt,
    conv_w,
    conv_b,
    dt_bias,
    a_log,
    d_skip,
    gate_gain,
    w_out,
    doc_lens,
    d_out,
):
    tp_count = lax.axis_size("tp")
    tp_rank = lax.axis_index("tp")
    dev_rows = x_in.shape[0]
    group_rows = dev_rows * tp_count
    head_count = dt_bias.shape[0]
    inner_width = gate_gain.shape[0]
    head_size = inner_width // head_count
    state_size = (conv_w.shape[0] - inner_width) // 2
    rim_rows = conv_w.shape[1] - 1
    col_widths = [w_z.shape[1], w_x.shape[1], w_b.shape[1], w_c.shape[1], w_dt.shape[1]]
    col_edges = [0]
    for col_width in col_widths:
        col_edges.append(col_edges[-1] + col_width)
    total_cols = col_edges[-1]
    contract_first = (((0,), (0,)), ((), ()))
    contract_last = (((1,), (1,)), ((), ()))
    lengths = doc_lens[0]
    doc_starts = jnp.cumsum(lengths) - lengths
    positions = tp_rank * dev_rows - rim_rows + jnp.arange(dev_rows + rim_rows, dtype=jnp.int32)
    seg_ext = jnp.sum((positions[:, None] >= doc_starts[None, :]).astype(jnp.int32), axis=1)
    seg_own = seg_ext[rim_rows:]
    seg_before = [seg_ext[rim_rows - 1]]
    x_float = x_in.astype(jnp.float32)
    normed = in_norm(x_float, norm_gain).astype(jnp.bfloat16)
    w_joined = jnp.concatenate([w_z, w_x, w_b, w_c, w_dt], axis=1)
    gathered = lax.all_gather(normed, "tp", axis=0, tiled=True)
    projected = jnp.dot(gathered, w_joined, preferred_element_type=jnp.float32).astype(jnp.bfloat16)
    padded = jnp.concatenate([jnp.zeros((rim_rows, total_cols), jnp.bfloat16), projected], axis=0)
    rims = padded[:group_rows].reshape(tp_count, dev_rows, total_cols)[:, :rim_rows]
    blocks = jnp.concatenate([rims, projected.reshape(tp_count, dev_rows, total_cols)], axis=1)
    arrived = lax.all_to_all(blocks, "tp", split_axis=0, concat_axis=2, tiled=True).reshape(
        dev_rows + rim_rows, tp_count, total_cols
    )

    def columns(source, which):
        return source[:, :, col_edges[which] : col_edges[which + 1]].reshape(source.shape[0], -1)

    gate_in = columns(arrived[rim_rows:], 0).astype(jnp.float32)
    conv_in = jnp.concatenate(
        [columns(arrived, 1), columns(arrived, 2), columns(arrived, 3)], axis=1
    ).astype(jnp.float32)
    dt_in = columns(arrived[rim_rows:], 4).astype(jnp.float32)

    def prepare(conv_in, dt_in, conv_w, conv_b, dt_bias, a_log):
        summed = jnp.zeros((dev_rows, conv_in.shape[1]), jnp.float32) + conv_b[None, :]
        for kernel_tap in range(conv_w.shape[1]):
            match = (seg_ext[kernel_tap : kernel_tap + dev_rows] == seg_own).astype(jnp.float32)
            summed = (
                summed
                + conv_w[:, kernel_tap][None, :]
                * conv_in[kernel_tap : kernel_tap + dev_rows]
                * match[:, None]
            )
        active = jax.nn.silu(summed)
        values = active[:, :inner_width].reshape(dev_rows, head_count, head_size)
        b_rows = active[:, inner_width : inner_width + state_size]
        c_rows = active[:, inner_width + state_size :]
        steps_dt = jax.nn.softplus(dt_in + dt_bias[None, :])
        log_decay = -steps_dt * jnp.exp(a_log)[None, :]
        return (values, b_rows, c_rows, log_decay, steps_dt)

    prepared, prepare_back = jax.vjp(prepare, conv_in, dt_in, conv_w, conv_b, dt_bias, a_log)
    values, b_rows, c_rows, log_decay, steps_dt = prepared

    def ssd_local(values, b_rows, c_rows, log_decay, steps_dt):
        state = jnp.zeros((head_count, head_size, state_size), jnp.float32)
        carried_all = jnp.ones((head_count,), jnp.float32)
        output, state, carried = span_pass(
            state, values, b_rows, c_rows, log_decay, steps_dt, seg_own, seg_before[0]
        )
        outputs = [output]
        carried_all = carried_all * carried
        return (jnp.concatenate(outputs, axis=0), carried_all, state)

    def entering(state_in, c_rows, log_decay):
        decay = jnp.ones((head_count,), jnp.float32)
        cumulative, inward, carried = span_parts(log_decay, seg_own, seg_before[0])
        reached = jnp.einsum(
            "tn,hpn->thp", c_rows, decay[:, None, None] * state_in, precision=HIGHEST
        )
        outputs = [reached * inward[:, :, None]]
        return jnp.concatenate(outputs, axis=0)

    identity = (
        jnp.ones((head_count,), jnp.float32),
        jnp.zeros((head_count, head_size, state_size), jnp.float32),
    )
    local_parts, ssd_back = jax.vjp(ssd_local, values, b_rows, c_rows, log_decay, steps_dt)
    local_out, carried_dev, state_dev = local_parts
    chained = entering_2((carried_dev, state_dev), "tp", combine, identity, False)
    state_in = chained[1]
    extra_out, entering_back = jax.vjp(entering, state_in, c_rows, log_decay)
    ssd_out = local_out + extra_out

    def gated(ssd_out, values, gate_in, d_skip, gate_gain):
        mixed_heads = ssd_out + d_skip[None, :, None] * values
        flat = mixed_heads.reshape(dev_rows, inner_width)
        gated_rows = flat * jax.nn.silu(gate_in)
        scale = lax.rsqrt(jnp.mean(gated_rows * gated_rows, axis=-1, keepdims=True) + EPSILON)
        return gated_rows * scale * gate_gain[None, :]

    normal_out, gated_back = jax.vjp(gated, ssd_out, values, gate_in, d_skip, gate_gain)
    rounded = normal_out.astype(jnp.bfloat16)
    by_heads = lax.all_to_all(rounded, "tp", split_axis=1, concat_axis=0, tiled=True)
    branch_out = lax.psum_scatter(
        jnp.dot(by_heads, w_out, preferred_element_type=jnp.float32),
        "tp",
        scatter_dimension=0,
        tiled=True,
    )
    block_out = (x_float + branch_out).astype(jnp.bfloat16)
    grad_gathered = lax.all_gather(d_out, "tp", axis=0, tiled=True)
    grad_heads = lax.dot_general(
        grad_gathered, w_out, contract_last, preferred_element_type=jnp.float32
    ).astype(jnp.bfloat16)
    grad_normal = lax.all_to_all(grad_heads, "tp", split_axis=0, concat_axis=1, tiled=True)
    grad_ssd, grad_values_a, grad_gate_in, grad_skip, grad_gate_gain = gated_back(
        grad_normal.astype(jnp.float32)
    )
    grad_state_in, grad_c_a, grad_decay_a = entering_back(grad_ssd)
    chained_back = entering_2((carried_dev, grad_state_in), "tp", combine, identity, True)
    grad_state_dev = chained_back[1]
    grad_carried = jnp.sum(grad_state_dev * state_in, axis=(1, 2))
    grad_values_b, grad_b, grad_c_b, grad_decay_b, grad_dt = ssd_back(
        (grad_ssd, grad_carried, grad_state_dev)
    )
    grad_conv_in, grad_dt_in, grad_conv_w, grad_conv_b, grad_dt_bias, grad_a_log = prepare_back(
        (
            grad_values_a + grad_values_b,
            grad_b,
            grad_c_a + grad_c_b,
            grad_decay_a + grad_decay_b,
            grad_dt,
        )
    )

    def split_heads(array):
        return array.reshape(array.shape[0], tp_count, -1)

    grad_gate_full = jnp.concatenate(
        [jnp.zeros((rim_rows, inner_width), jnp.float32), grad_gate_in], axis=0
    )
    grad_dt_full = jnp.concatenate(
        [jnp.zeros((rim_rows, head_count), jnp.float32), grad_dt_in], axis=0
    )
    pieces = [
        split_heads(grad_gate_full),
        split_heads(grad_conv_in[:, :inner_width]),
        split_heads(grad_conv_in[:, inner_width : inner_width + state_size]),
        split_heads(grad_conv_in[:, inner_width + state_size :]),
        split_heads(grad_dt_full),
    ]
    outgoing = jnp.concatenate(pieces, axis=2).reshape(
        1, dev_rows + rim_rows, tp_count * total_cols
    )
    returned = lax.all_to_all(outgoing, "tp", split_axis=2, concat_axis=0, tiled=True)
    main_rows = returned[:, rim_rows:]
    main_rows = main_rows.at[:-1, dev_rows - rim_rows :].add(returned[1:, :rim_rows])
    grad_projected = main_rows.reshape(group_rows, total_cols).astype(jnp.bfloat16)
    grad_normed = lax.psum_scatter(
        lax.dot_general(
            grad_projected, w_joined, contract_last, preferred_element_type=jnp.float32
        ),
        "tp",
        scatter_dimension=0,
        tiled=True,
    )
    _, norm_back = jax.vjp(in_norm, x_float, norm_gain)
    grad_x_norm, grad_norm_gain = norm_back(grad_normed)
    grad_x = d_out.astype(jnp.float32) + grad_x_norm
    in_part = lax.dot_general(
        gathered, grad_projected, contract_first, preferred_element_type=jnp.float32
    )
    weight_grads = lax.psum_scatter(
        jnp.concatenate(
            [
                in_part,
                lax.dot_general(
                    grad_gathered, by_heads, contract_first, preferred_element_type=jnp.float32
                ),
            ],
            axis=1,
        ),
        "dp",
        scatter_dimension=0,
        tiled=True,
    )
    grad_w_z = weight_grads[:, col_edges[0] : col_edges[1]]
    grad_w_x = weight_grads[:, col_edges[1] : col_edges[2]]
    grad_w_b = weight_grads[:, col_edges[2] : col_edges[3]]
    grad_w_c = weight_grads[:, col_edges[3] : col_edges[4]]
    grad_w_dt = weight_grads[:, col_edges[4] : col_edges[5]]
    grad_w_out = weight_grads[:, total_cols:].T
    summed_small = lax.psum(
        (
            grad_norm_gain,
            grad_conv_w,
            grad_conv_b,
            grad_dt_bias,
            grad_a_log,
            grad_skip,
            grad_gate_gain,
        ),
        ("dp", "tp"),
    )
    return (
        block_out,
        grad_x,
        summed_small[0],
        grad_w_z,
        grad_w_x,
        grad_w_b,
        grad_w_c,
        grad_w_dt,
        summed_small[1],
        summed_small[2],
        summed_small[3],
        summed_small[4],
        summed_small[5],
        summed_small[6],
        grad_w_out,
    )


def solution(mesh):
    placed = (
        P(("dp", "tp"), None),
        P(),
        P(None, "tp"),
        P(None, "tp"),
        P(None, "tp"),
        P(None, "tp"),
        P(None, "tp"),
        P(),
        P(),
        P(),
        P(),
        P(),
        P(),
        P("tp", None),
        P("dp", None),
        P(("dp", "tp"), None),
    )
    return jax.shard_map(
        body,
        mesh=mesh,
        in_specs=placed,
        out_specs=(
            P(("dp", "tp"), None),
            P(("dp", "tp"), None),
            P(),
            P("dp", "tp"),
            P("dp", "tp"),
            P("dp", "tp"),
            P("dp", "tp"),
            P("dp", "tp"),
            P(),
            P(),
            P(),
            P(),
            P(),
            P(),
            P("tp", "dp"),
        ),
        check_vma=False,
    )
```

profile of v0, /device:TPU:1, one launch (start us, length us, event | category | flops | bytes accessed | tf_op | source)
XLA Modules:
  0.0 1443.4 jit_solution(17318158812077434221)
XLA Ops:
  12.3 14.3 concatenate.29
  26.6 39.8 %all-gather.8.cloned.1.call-done = bf16[1024,2048]{1,0:T(8,128)(2,1)} async-done(((bf16[256,2048]{1,0:T(8,128)(2,1)}), bf16[1024,2048]{1,0:T(8,128)(2,1)}) %all-gather.8.cloned.1.call-update) | async-done | bytes 4194320 | tf_op jit(solution)/shard_map/all_gather | solution.py:115
  66.3 13.6 convolution_convert_fusion
  86.6 6.4 copy.204
  93.1 6.4 copy.203
  117.4 60.6 %all-to-all-done = bf16[4,259,2128]{2,1,0:T(8,128)(2,1)} async-done(((bf16[4,259,2128]{2,1,0:T(8,128)(2,1)}), bf16[4,259,2128]{2,1,0:T(8,128)(2,1)}, u32[]{:S(2)}, u32[]{:S(2)}) %all-to-all-start) | async-done | bytes 4409248 | tf_op jit(solution)/shard_map/all_to_all | solution.py:120
  178.0 8.2 copy.176
  218.3 7.0 fusion.78
  225.4 8.0 convolution_convert_fusion.1
  240.8 43.3 %all-to-all-done.2 = bf16[4,256,1024]{1,2,0:T(8,128)(2,1)} async-done(((bf16[4,256,1024]{1,2,0:T(8,128)(2,1)}), bf16[4,256,1024]{1,2,0:T(8,128)(2,1)}, u32[]{:S(2)}, u32[]{:S(2)}) %all-to-all-start.2) | async-done | bytes 2097184 | tf_op jit(solution)/shard_map/all_to_all | solution.py:205
  288.1 6.3 all-gather.2
  295.7 6.2 fusion.92
  305.8 32.7 %all-gather.12.cloned.1.call-done = f32[256,64,128]{2,1,0:T(8,128)} async-done(((f32[64,64,128]{2,1,0:T(8,128)}), f32[256,64,128]{2,1,0:T(8,128)}) %all-gather.12.cloned.1.call-update) | async-done | bytes 8388624 | tf_op jit(solution)/shard_map/all_gather | solution.py:12
  338.5 8.5 while.31
  351.5 23.6 %multiply_reduce_fusion.11 = (f32[256]{0:T(256)S(1)}, f32[256,64,64]{0,2,1:T(8,128)S(1)}, f32[256,64,64]{0,2,1:T(8,128)}) fusion(f32[256,64,64]{0,2,1:T(8,128)} %bitcast.311, f32[256,64,64]{0,2,1:T(8,128)S(1)} %bitcast.299, f32[64]{0:T(128)S(1)} %copy-done.73, f32[256,64,64]{0,2,1:T(8,128)S(1)} %fusion.100, f32[256,64,64]{0,2,1:T(8,128)} %fusion.92, ...), kind=kOutput, calls=%fused_computation.87 | convolution fusion | flops 3251633920 | bytes 25691392 | tf_op jit(solution)/shard_map/jvp(tsh,shp->thp)/dot_general | solution.py:44
  377.4 6.0 multiply_reduce_fusion.6
  403.4 7.6 copy.193
  411.0 8.8 fusion.84
  419.8 6.7 fusion.81
  426.6 26.2 %fusion.10 = (f32[256,64]{0,1:T(8,128)S(1)}, f32[256,64]{0,1:T(8,128)S(1)}, f32[256,64]{0,1:T(8,128)}, f32[256,256]{1,0:T(8,128)S(1)}) fusion(f32[256,64]{0,1:T(8,128)S(1)} %copy-done.43, f32[256,256]{1,0:T(8,128)S(1)} %copy-done.23, f32[256,64]{0,1:T(8,128)S(1)} %bitcast_bitcast_fusion.1, pred[256,256]{1,0:T(8,128)(4,1)S(1)} %fusion.95, ...), kind=kOutput, calls=%fused_computation.18 | convolution fusion | flops 3275636736 | bytes 9306112 | tf_op jit(solution)/shard_map/transpose(jvp(tsh,shp->thp))/dot_general | solution.py:44
  454.0 24.7 %all-gather.14.cloned.1.call-done = f32[256,64,128]{2,1,0:T(8,128)} async-done(((f32[64,64,128]{2,1,0:T(8,128)}), f32[256,64,128]{2,1,0:T(8,128)}) %all-gather.14.cloned.1.call-update) | async-done | bytes 8388624 | tf_op jit(solution)/shard_map/all_gather | solution.py:12
  478.7 14.9 %while.32 = (s32[]{:T(128)}, f32[64,64,128]{2,1,0:T(8,128)}, s32[]{:T(128)}, f32[4,64]{1,0:T(4,128)S(1)}, f32[4,64,64,128]{3,2,1,0:T(8,128)}, /*index=5*/s32[]{:T(128)}, s32[]{:T(128)}, s32[]{:T(128)}, s32[]{:T(128)}) while((s32[]{:T(128)}, f32[64,64,128]{2,1,0:T(8,128)}, s32[]{:T(128)}, f32[4,64]{1,0:T(4,128)S(1)}, ...), condition=%wide.region_12.13_spmd.clone, body=%wide.region_11.12_spmd.clone.sunk | while | flops 2097160 | bytes 6292391 | solution.py:25
  493.6 9.8 fusion.87
  510.5 15.7 %fusion.31 = f32[256,64,64]{0,2,1:T(8,128)} fusion(f32[256,64,64]{0,2,1:T(8,128)S(1)} %get-tuple-element.469, f32[256,64,64]{0,2,1:T(8,128)S(1)} %copy-done.7, f32[64]{0:T(128)S(1)} %copy-done.73, f32[256,64]{0,1:T(8,128)S(1)} %get-tuple-element.456, f32[256,64]{0,1:T(8,128)S(1)} %copy-done.43, f32[256,256]{1,0:T(8,128)S(1)} %copy-done.24, ...), kind=kOutput, calls=%fused_computation.58 | convolution fusion | flops 3242196992 | bytes 13107456 | tf_op jit(solution)/shard_map/transpose(jvp(tsh,shp->thp))/dot_general | solution.py:44
  526.2 6.0 copy.185
  532.2 12.2 multiply_reduce_fusion.4
  549.5 7.2 pad_add_fusion
  566.3 6.1 reshape.445
  572.4 15.8 %concatenate.35 = f32[259,4,2128]{2,1,0:T(4,128)} concatenate(f32[259,4,1024]{2,1,0:T(4,128)} %copy.193, f32[259,4,1024]{2,1,0:T(4,128)} %reshape.445, f32[259,4,32]{2,1,0:T(4,128)S(1)} %copy.194, f32[259,4,32]{2,1,0:T(4,128)S(1)} %copy.195, f32[259,4,16]{2,1,0:T(4,128)S(1)} %copy.196), dimensions={2} | concatenate | bytes 17636864 | tf_op jit(solution)/shard_map/concatenate | solution.py:242
  588.2 11.4 reshape.454
  599.6 27.3 %copy.197 = f32[1,259,8512]{1,0,2:T(1,128)} copy(f32[1,259,8512]{2,1,0:T(8,128)} %reshape.454) | data formatting | bytes 17636864 | tf_op jit(solution)/shard_map/reshape | solution.py:242
  626.8 6.5 all-to-all-start.3
  634.7 140.7 %all-to-all-done.3 = f32[1,259,8512]{1,0,2:T(1,128)} async-done(((f32[1,259,8512]{1,0,2:T(1,128)}), f32[1,259,8512]{1,0,2:T(1,128)}, u32[]{:S(2)}, u32[]{:S(2)}) %all-to-all-start.3) | async-done | bytes 8818464 | tf_op jit(solution)/shard_map/all_to_all | solution.py:245
  775.4 11.9 copy.207
  787.3 7.0 slice.233
  802.5 22.9 %scatter-add.4 = f32[4,256,2128]{1,2,0:T(8,128)} dynamic-update-slice(f32[4,256,2128]{1,2,0:T(8,128)} %copy-done.8, f32[3,3,2128]{1,2,0:T(8,128)S(1)} %add_select_fusion, s32[]{:T(128)} %bitcast.52, s32[]{:T(128)} %bitcast.53, s32[]{:T(128)} %constant.140.clone.1) | dynamic-update-slice | bytes 153220 | tf_op jit(solution)/shard_map/scatter-add | solution.py:247
  825.4 5.9 convert_element_type.125
  831.3 6.4 copy.200
  837.7 15.7 %fusion.148 = f32[1024,2048]{1,0:T(8,128)} fusion(bf16[1024,2128]{1,0:T(8,128)(2,1)} %bitcast.319, bf16[2048,2128]{1,0:T(8,128)(2,1)} %concatenate.29), kind=kOutput, calls=%fused_computation.237 | convolution fusion | flops 8925478912 | bytes 21463040 | tf_op jit(solution)/shard_map/dot_general | solution.py:250
  857.8 49.7 %all_to_all.62 = bf16[256,4,1024]{0,2,1:T(8,128)(2,1)S(1)} all-to-all(bf16[256,4,1024]{0,2,1:T(8,128)(2,1)S(1)} %fusion.48), channel_id=1, replica_groups=mesh['dp'=8,'tp'=4] {'tp'}, dimensions={1} | all-to-all | bytes 4194304 | tf_op jit(solution)/shard_map/all_to_all | solution.py:193
  909.9 10.7 fusion.147
  922.2 9.1 convolution_bitcast_fusion
  931.3 12.9 fusion.149
  944.2 16.0 %pad_maximum_fusion = f32[2048,3152]{0,1:T(8,128)} fusion(f32[2048,1024]{0,1:T(8,128)} %convolution_bitcast_fusion, f32[2048,2128]{0,1:T(8,128)S(1)} %fusion.149), kind=kLoop, calls=%fused_computation.6 | loop fusion | flops 6455296 | bytes 51642368 | tf_op jit(solution)/shard_map/concatenate | solution.py:264
  965.7 41.9 %all-reduce.16 = (f32[2048]{0:T(1024)}, f32[4352]{0:T(1024)}, f32[64]{0:T(128)}, f32[64]{0:T(128)}, f32[64]{0:T(128)}, /*index=5*/f32[4096]{0:T(1024)}) all-reduce(f32[2048]{0:T(1024)S(1)} %get-tuple-element.395, f32[4352]{0:T(1024)S(1)} %copy-done.32, f32[64]{0:T(128)S(1)} %get-tuple-element.431, ...), channel_id=1, replica_groups=mesh['dp'=8,'tp'=4] {'dp','tp'}, use_global_device_ids=true, to_apply=%region_30.31 | all-reduce | flops 10688 | bytes 85504 | tf_op jit(solution)/shard_map/psum | solution.py:283
  1007.6 46.4 %reduce-scatter.4.cloned.1.call-done = f32[256,2048]{1,0:T(8,128)} async-done(((f32[1024,2048]{1,0:T(8,128)}), f32[256,2048]{1,0:T(8,128)}) %reduce-scatter.4.cloned.1.call-update) | async-done | bytes 2097168 | tf_op jit(solution)/shard_map/reduce_scatter | solution.py:194
  1058.3 249.3 %reduce-scatter.8.cloned.1.call-done = f32[256,3152]{0,1:T(8,128)} async-done(((f32[2048,3152]{0,1:T(8,128)}), f32[256,3152]{0,1:T(8,128)}) %reduce-scatter.8.cloned.1.call-update) | async-done | bytes 3227664 | tf_op jit(solution)/shard_map/reduce_scatter | solution.py:263
  1316.0 118.6 %all-reduce.19.cloned.1.call-done = f32[4352,4]{0,1:T(4,128)} async-done(((f32[4352,4]{0,1:T(4,128)}), f32[4352,4]{0,1:T(4,128)}) %all-reduce.19.cloned.1.call-update) | async-done | bytes 69648 | tf_op jit(solution)/shard_map/psum | solution.py:283
  (293 shorter events, 186.9 us)
Async XLA Ops:
  7.2 59.1 %all-gather.8.cloned.1.call-start = ((), (), s32[]{:S(2)}) async-start(), calls=%async_computation.7 | async-start | bytes 5242880 | tf_op jit(solution)/shard_map/all_gather | solution.py:115
  106.0 6.4 copy-start.74
  106.0 6.4 copy-start.72
  106.0 8.6 copy-start.38
  106.0 72.0 %all-to-all-start = ((bf16[4,259,2128]{2,1,0:T(8,128)(2,1)}), bf16[4,259,2128]{2,1,0:T(8,128)(2,1)}, u32[]{:S(2)}, u32[]{:S(2)}) async-start(bf16[4,259,2128]{2,1,0:T(8,128)(2,1)} %pad_maximum_fusion.1), calls=%async_computation | async-start | bytes 9191424 | tf_op jit(solution)/shard_map/all_to_all | solution.py:120
  111.1 114.3 %all-gather.10.cloned.1.call-start = ((), (), s32[]{:S(2)}) async-start(), calls=%async_computation.9 | async-start | bytes 5242880 | tf_op jit(solution)/shard_map/all_gather | solution.py:201
  111.8 226.7 %all-gather.12.cloned.1.call-start = ((), (), s32[]{:S(2)}) async-start(), calls=%async_computation.13 | async-start | bytes 10485760 | tf_op jit(solution)/shard_map/all_gather | solution.py:12
  112.4 80.9 %copy-start.68 = (f32[64]{0:T(128)}, f32[64]{0:T(128)S(1)}, u32[]{:S(2)}) copy-start(f32[64]{0:T(128)S(1)} %exp.58) | copy-start | bytes 772
  112.7 73.5 %copy-start.45 = (s32[259]{0:T(512)}, s32[259]{0:T(512)S(1)}, u32[]{:S(2)}) copy-start(s32[259]{0:T(512)S(1)} %convert_reduce_fusion) | copy-start | bytes 3112
  186.2 7.2 copy-start.59
  193.4 24.8 %copy-start.20 = (bf16[256,4,16]{0,2,1:T(8,128)(2,1)}, bf16[256,4,16]{0,2,1:T(8,128)(2,1)S(1)}, u32[]{:S(2)}) copy-start(bf16[256,4,16]{0,2,1:T(8,128)(2,1)S(1)} %slice.224) | copy-start | bytes 98308
  212.0 6.1 copy-start.50
  212.0 6.1 copy-start.60
  212.0 6.1 copy-start.64
  218.1 7.2 copy-start.62
  218.3 133.2 %copy-start.42 = (f32[256,64]{0,1:T(8,128)}, f32[256,64]{0,1:T(8,128)S(1)}, u32[]{:S(2)}) copy-start(f32[256,64]{0,1:T(8,128)S(1)} %get-tuple-element.457) | copy-start | bytes 196612
  233.4 7.2 copy-start.46
  233.4 7.2 copy-start.27
  236.0 48.2 %all-to-all-start.2 = ((bf16[4,256,1024]{1,2,0:T(8,128)(2,1)}), bf16[4,256,1024]{1,2,0:T(8,128)(2,1)}, u32[]{:S(2)}, u32[]{:S(2)}) async-start(bf16[4,256,1024]{1,2,0:T(8,128)(2,1)} %copy.184), calls=%async_computation.3 | async-start | bytes 4194304 | tf_op jit(solution)/shard_map/all_to_all | solution.py:205
  240.5 238.3 %all-gather.14.cloned.1.call-start = ((), (), s32[]{:S(2)}) async-start(), calls=%async_computation.14 | async-start | bytes 10485760 | tf_op jit(solution)/shard_map/all_gather | solution.py:12
  240.8 185.7 %copy-start.40 = (pred[256,256]{1,0:T(8,128)(4,1)}, pred[256,256]{1,0:T(8,128)(4,1)S(1)}, u32[]{:S(2)}) copy-start(pred[256,256]{1,0:T(8,128)(4,1)S(1)} %fusion.95) | copy-start | bytes 196612
  295.7 55.8 %copy-start.22 = (f32[256,256]{1,0:T(8,128)}, f32[256,256]{1,0:T(8,128)S(1)}, u32[]{:S(2)}) copy-start(f32[256,256]{1,0:T(8,128)S(1)} %fusion.106) | copy-start | bytes 786436
  351.5 23.7 %copy-start.16 = (f32[256,64,64]{0,2,1:T(8,128)}, f32[256,64,64]{0,2,1:T(8,128)S(1)}, u32[]{:S(2)}) copy-start(f32[256,64,64]{0,2,1:T(8,128)S(1)} %fusion.100) | copy-start | bytes 12582916
  351.5 23.6 %copy-start.11 = (f32[4,256,1024]{1,2,0:T(8,128)S(1)}, f32[4,256,1024]{1,2,0:T(8,128)}, u32[]{:S(2)}) copy-start(f32[4,256,1024]{1,2,0:T(8,128)} %convert_element_type.132) | copy-start | bytes 12582916
  375.1 18.6 %copy-start.47 = (f32[256]{0:T(256)}, f32[256]{0:T(256)S(1)}, u32[]{:S(2)}) copy-start(f32[256]{0:T(256)S(1)} %fusion.132) | copy-start | bytes 3076
  411.0 8.8 copy-start.6
  419.8 6.7 copy-start.3
  419.8 6.7 copy-start.23
  419.8 6.7 copy-start.43
  493.6 9.9 copy-start.1
  493.6 9.9 copy-start.4
  526.2 6.0 copy-start.52
  526.2 6.0 copy-start.54
  526.2 6.0 copy-start.56
  549.4 7.2 copy-start.21
  549.4 7.2 copy-start.61
  549.4 7.2 copy-start.63
  549.4 7.2 copy-start.65
  549.4 10.6 copy-start.44
  549.5 10.6 copy-start.69
  626.8 7.1 copy-start.71
  626.8 148.5 %all-to-all-start.3 = ((f32[1,259,8512]{1,0,2:T(1,128)}), f32[1,259,8512]{1,0,2:T(1,128)}, u32[]{:S(2)}, u32[]{:S(2)}) async-start(f32[1,259,8512]{1,0,2:T(1,128)} %copy.197), calls=%async_computation.4 | async-start | bytes 26148864 | tf_op jit(solution)/shard_map/all_to_all | solution.py:245
  633.3 329.9 %reduce-scatter.6.cloned.1.call-start = ((), (), s32[]{:S(2)}) async-start(), calls=%async_computation.10 | async-start | bytes 10485760 | tf_op jit(solution)/shard_map/reduce_scatter | solution.py:249
  853.5 200.5 %reduce-scatter.4.cloned.1.call-start = ((), (), s32[]{:S(2)}) async-start(), calls=%async_computation.8 | async-start | bytes 10485760 | tf_op jit(solution)/shard_map/reduce_scatter | solution.py:194
  920.6 387.0 %reduce-scatter.8.cloned.1.call-start = ((), (), s32[]{:S(2)}) async-start(), calls=%async_computation.11 | async-start | bytes 29048832 | tf_op jit(solution)/shard_map/reduce_scatter | solution.py:263
  960.3 5.4 copy-start.32
  960.3 474.2 %all-reduce.19.cloned.1.call-start = ((), (), s32[]{:S(2)}) async-start(), calls=%async_computation.12 | async-start | bytes 139264 | tf_op jit(solution)/shard_map/psum | solution.py:283
  963.3 90.7 %copy-start.18 = (f32[256,2048]{1,0:T(8,128)S(1)}, f32[256,2048]{1,0:T(8,128)}, u32[]{:S(2)}) copy-start(f32[256,2048]{1,0:T(8,128)} %reduce-scatter.6.cloned.1.call-done) | copy-start | bytes 6291460
  (39 other events, 99.8 us)
Sparse Core Ops, SparseCore 0:
  11.5 54.7 all-gather.7
  113.7 83.3 all-gather.9
  225.4 113.0 all-gather.11
  391.1 87.6 all-gather.13
  853.6 109.6 reduce-scatter.5
  966.5 87.4 reduce-scatter.3
  1056.3 251.1 reduce-scatter.7
  1314.7 119.8 all-reduce.18
where the time goes:
time: 1460 us; the launch traced here: 1440 us
  waiting for transfers between devices  758 us (52%)
  local copies, waits for them, and re-layouts  230 us (16%)
  matrix products  193 us (13%)
  other arithmetic  130 us (9%)
  blocking collectives  97.8 us (7%)
  between operations  17.1 us (1%)
  starting transfers between devices  16.9 us (1%)
    reduce_scatter x1, waiting for transfers between devices, body(): lax.psum_scatter(jnp.concatenate([in_part, lax.dot_general(grad_gathered,...  249 us
    all_to_all x1, waiting for transfers between devices, body(): lax.all_to_all(outgoing, 'tp', split_axis=2, concat_axis=0, tiled=True)  141 us
    psum x1, waiting for transfers between devices, body(): lax.psum((grad_norm_gain, grad_conv_w, grad_conv_b, grad_dt_bias, grad_a_...  119 us
    dot_general x3, matrix products, span_pass(): output = jnp.einsum('tsh,shp->thp', mixing, values, precision=HIGHEST)  65.4 us
    all_to_all x1, waiting for transfers between devices, body(): lax.all_to_all(blocks, 'tp', split_axis=0, concat_axis=2, tiled=True)  60.6 us
    all_gather x2, waiting for transfers between devices, entering_2(): everything = jax.tree.map(lambda part: lax.all_gather(part, axis), array)  57.4 us
    all_to_all x1, blocking collectives, body(): lax.all_to_all(rounded, 'tp', split_axis=1, concat_axis=0, tiled=True)  49.7 us
    reduce_scatter x1, waiting for transfers between devices, body(): lax.psum_scatter(jnp.dot(by_heads, w_out, preferred_element_type=jnp.floa...  46.4 us
  transfers between devices with their start and end apart: 11, of which 10 were waited for; matrix products, arithmetic and copies ran while one was open for 15% of the time, Pallas kernels for 0%

commit v1 on v0

--- a/solution.py
+++ b/solution.py
@@ -281,16 +281,19 @@
     grad_w_dt = weight_grads[:, col_edges[4] : col_edges[5]]
     grad_w_out = weight_grads[:, total_cols:].T
     summed_small = lax.psum(
-        (
-            grad_norm_gain,
-            grad_conv_w,
-            grad_conv_b,
-            grad_dt_bias,
-            grad_a_log,
-            grad_skip,
-            grad_gate_gain,
+        lax.psum(
+            (
+                grad_norm_gain,
+                grad_conv_w,
+                grad_conv_b,
+                grad_dt_bias,
+                grad_a_log,
+                grad_skip,
+                grad_gate_gain,
+            ),
+            "tp",
         ),
-        ("dp", "tp"),
+        "dp",
     )
     return (
         block_out,

time: 1460 us -> 1390 us (0.952)
  waiting for transfers between devices: 758 us -> 688 us
    psum x1, waiting for transfers between devices: 119 us -> 0.02 us  [body(): lax.psum((grad_norm_gain, grad_conv_w, grad_conv_b, grad_dt_bias, grad_a_...]
    psum x0 -> x1, waiting for transfers between devices: none -> 44.8 us  [body(): lax.psum(lax.psum((grad_norm_gain, grad_conv_w, grad_conv_b, grad_dt_bias...]
    psum x1, blocking collectives: 41.9 us -> 13.2 us  [body(): lax.psum((grad_norm_gain, grad_conv_w, grad_conv_b, grad_dt_bias, grad_a_...]
    psum x0 -> x1, blocking collectives: none -> 27.7 us  [body(): lax.psum(lax.psum((grad_norm_gain, grad_conv_w, grad_conv_b, grad_dt_bias...]
    unnamed x159 -> x135, local copies, waits for them, and re-layouts: 35 us -> 33.4 us
  transfers between devices with their start and end apart: 11 -> 12, of which waited for: 10 -> 10; matrix products, arithmetic and copies ran while one was open for 15% -> 22% of each run, Pallas kernels for 0% -> 0%
where the time goes in v1:
time: 1390 us; the launch traced here: 1380 us
  waiting for transfers between devices  688 us (49%)
  local copies, waits for them, and re-layouts  232 us (17%)
  matrix products  191 us (14%)
  other arithmetic  133 us (10%)
  blocking collectives  97.3 us (7%)
  starting transfers between devices  17 us (1%)
  between operations  16.7 us (1%)
    reduce_scatter x1, waiting for transfers between devices, body(): lax.psum_scatter(jnp.concatenate([in_part, lax.dot_general(grad_gathered,...  249 us
    all_to_all x1, waiting for transfers between devices, body(): lax.all_to_all(outgoing, 'tp', split_axis=2, concat_axis=0, tiled=True)  141 us
    dot_general x3, matrix products, span_pass(): output = jnp.einsum('tsh,shp->thp', mixing, values, precision=HIGHEST)  65.5 us
    all_to_all x1, waiting for transfers between devices, body(): lax.all_to_all(blocks, 'tp', split_axis=0, concat_axis=2, tiled=True)  61.8 us
    all_gather x2, waiting for transfers between devices, entering_2(): everything = jax.tree.map(lambda part: lax.all_gather(part, axis), array)  57.1 us
    all_to_all x1, blocking collectives, body(): lax.all_to_all(rounded, 'tp', split_axis=1, concat_axis=0, tiled=True)  50.2 us
    reduce_scatter x1, waiting for transfers between devices, body(): lax.psum_scatter(jnp.dot(by_heads, w_out, preferred_element_type=jnp.floa...  47 us
    psum x1, waiting for transfers between devices, body(): lax.psum(lax.psum((grad_norm_gain, grad_conv_w, grad_conv_b, grad_dt_bias...  44.8 us
  transfers between devices with their start and end apart: 12, of which 10 were waited for; matrix products, arithmetic and copies ran while one was open for 22% of the time, Pallas kernels for 0%

profile of v1, /device:TPU:1, one launch (start us, length us, event | category | flops | bytes accessed | tf_op | source)
XLA Modules:
  0.0 1375.8 jit_solution(6411934169579836168)
XLA Ops:
  12.3 14.3 %concatenate.29 = bf16[2048,2128]{1,0:T(8,128)(2,1)} concatenate(bf16[2048,1024]{1,0:T(8,128)(2,1)} %param.24, bf16[2048,1024]{1,0:T(8,128)(2,1)} %param.25, bf16[2048,32]{1,0:T(8,128)(2,1)S(1)} %copy.171, bf16[2048,32]{1,0:T(8,128)(2,1)S(1)} %copy.172, bf16[2048,16]{1,0:T(8,128)(2,1)S(1)} %copy.173), dimensions={1} | concatenate | bytes 17432576 | tf_op jit(solution)/shard_map/concatenate | solution.py:114
  26.6 39.8 %all-gather.8.cloned.1.call-done = bf16[1024,2048]{1,0:T(8,128)(2,1)} async-done(((bf16[256,2048]{1,0:T(8,128)(2,1)}), bf16[1024,2048]{1,0:T(8,128)(2,1)}) %all-gather.8.cloned.1.call-update) | async-done | bytes 4194320 | tf_op jit(solution)/shard_map/all_gather | solution.py:115
  66.3 13.6 convolution_convert_fusion
  86.6 6.4 copy.204
  93.1 6.4 copy.203
  116.2 61.8 %all-to-all-done = bf16[4,259,2128]{2,1,0:T(8,128)(2,1)} async-done(((bf16[4,259,2128]{2,1,0:T(8,128)(2,1)}), bf16[4,259,2128]{2,1,0:T(8,128)(2,1)}, u32[]{:S(2)}, u32[]{:S(2)}) %all-to-all-start) | async-done | bytes 4409248 | tf_op jit(solution)/shard_map/all_to_all | solution.py:120
  178.0 8.2 copy.176
  221.5 6.9 fusion.78
  228.5 8.0 convolution_convert_fusion.1
  244.0 43.3 %all-to-all-done.2 = bf16[4,256,1024]{1,2,0:T(8,128)(2,1)} async-done(((bf16[4,256,1024]{1,2,0:T(8,128)(2,1)}), bf16[4,256,1024]{1,2,0:T(8,128)(2,1)}, u32[]{:S(2)}, u32[]{:S(2)}) %all-to-all-start.2) | async-done | bytes 2097184 | tf_op jit(solution)/shard_map/all_to_all | solution.py:205
  291.2 6.3 all-gather.2
  298.8 6.2 fusion.92
  308.8 32.8 %all-gather.12.cloned.1.call-done = f32[256,64,128]{2,1,0:T(8,128)} async-done(((f32[64,64,128]{2,1,0:T(8,128)}), f32[256,64,128]{2,1,0:T(8,128)}) %all-gather.12.cloned.1.call-update) | async-done | bytes 8388624 | tf_op jit(solution)/shard_map/all_gather | solution.py:12
  341.7 8.5 while.31
  354.7 23.6 %multiply_reduce_fusion.11 = (f32[256]{0:T(256)S(1)}, f32[256,64,64]{0,2,1:T(8,128)S(1)}, f32[256,64,64]{0,2,1:T(8,128)}) fusion(f32[256,64,64]{0,2,1:T(8,128)} %bitcast.311, f32[256,64,64]{0,2,1:T(8,128)S(1)} %bitcast.299, f32[64]{0:T(128)S(1)} %copy-done.61, f32[256,64,64]{0,2,1:T(8,128)S(1)} %fusion.100, f32[256,64,64]{0,2,1:T(8,128)} %fusion.92, ...), kind=kOutput, calls=%fused_computation.87 | convolution fusion | flops 3251633920 | bytes 25691392 | tf_op jit(solution)/shard_map/jvp(tsh,shp->thp)/dot_general | solution.py:44
  380.5 6.1 multiply_reduce_fusion.6
  407.0 7.6 copy.193
  414.6 8.8 fusion.84
  423.4 6.7 fusion.81
  430.1 26.3 %fusion.10 = (f32[256,64]{0,1:T(8,128)}, f32[256,64]{0,1:T(8,128)}, f32[256,64]{0,1:T(8,128)}, f32[256,256]{1,0:T(8,128)S(1)}) fusion(f32[256,64]{0,1:T(8,128)S(1)} %get-tuple-element.463, f32[256,256]{1,0:T(8,128)S(1)} %copy-done.22, f32[256,64]{0,1:T(8,128)S(1)} %bitcast_bitcast_fusion.1, pred[256,256]{1,0:T(8,128)(4,1)S(1)} %fusion.95, ...), kind=kOutput, calls=%fused_computation.18 | convolution fusion | flops 3275636736 | bytes 9306112 | tf_op jit(solution)/shard_map/transpose(jvp(tsh,shp->thp))/dot_general | solution.py:44
  457.7 24.2 %all-gather.14.cloned.1.call-done = f32[256,64,128]{2,1,0:T(8,128)} async-done(((f32[64,64,128]{2,1,0:T(8,128)}), f32[256,64,128]{2,1,0:T(8,128)}) %all-gather.14.cloned.1.call-update) | async-done | bytes 8388624 | tf_op jit(solution)/shard_map/all_gather | solution.py:12
  481.9 14.9 %while.32 = (s32[]{:T(128)}, f32[64,64,128]{2,1,0:T(8,128)}, s32[]{:T(128)}, f32[4,64]{1,0:T(4,128)S(1)}, f32[4,64,64,128]{3,2,1,0:T(8,128)}, /*index=5*/s32[]{:T(128)}, s32[]{:T(128)}, s32[]{:T(128)}, s32[]{:T(128)}) while((s32[]{:T(128)}, f32[64,64,128]{2,1,0:T(8,128)}, s32[]{:T(128)}, f32[4,64]{1,0:T(4,128)S(1)}, ...), condition=%wide.region_12.13_spmd.clone, body=%wide.region_11.12_spmd.clone.sunk | while | flops 2097160 | bytes 6292391 | solution.py:25
  496.8 9.9 fusion.87
  514.1 15.6 %fusion.31 = f32[256,64,64]{0,2,1:T(8,128)} fusion(f32[256,64,64]{0,2,1:T(8,128)S(1)} %get-tuple-element.475, f32[256,64,64]{0,2,1:T(8,128)S(1)} %copy-done.7, f32[64]{0:T(128)S(1)} %copy-done.61, f32[256,64]{0,1:T(8,128)S(1)} %get-tuple-element.462, f32[256,64]{0,1:T(8,128)S(1)} %get-tuple-element.463, f32[256,256]{1,0:T(8,128)S(1)} %copy-done.23, ...), kind=kOutput, calls=%fused_computation.58 | convolution fusion | flops 3242196992 | bytes 13107456 | tf_op jit(solution)/shard_map/transpose(jvp(tsh,shp->thp))/dot_general | solution.py:44
  535.8 12.3 multiply_reduce_fusion.4
  554.0 7.2 pad_add_fusion
  570.9 6.1 reshape.445
  577.0 15.8 %concatenate.35 = f32[259,4,2128]{2,1,0:T(4,128)} concatenate(f32[259,4,1024]{2,1,0:T(4,128)} %copy.193, f32[259,4,1024]{2,1,0:T(4,128)} %reshape.445, f32[259,4,32]{2,1,0:T(4,128)S(1)} %copy.194, f32[259,4,32]{2,1,0:T(4,128)S(1)} %copy.195, f32[259,4,16]{2,1,0:T(4,128)S(1)} %copy.196), dimensions={2} | concatenate | bytes 17636864 | tf_op jit(solution)/shard_map/concatenate | solution.py:242
  592.8 11.4 reshape.454
  604.2 27.3 %copy.197 = f32[1,259,8512]{1,0,2:T(1,128)} copy(f32[1,259,8512]{2,1,0:T(8,128)} %reshape.454) | data formatting | bytes 17636864 | tf_op jit(solution)/shard_map/reshape | solution.py:242
  631.5 6.5 all-to-all-start.3
  640.2 140.7 %all-to-all-done.3 = f32[1,259,8512]{1,0,2:T(1,128)} async-done(((f32[1,259,8512]{1,0,2:T(1,128)}), f32[1,259,8512]{1,0,2:T(1,128)}, u32[]{:S(2)}, u32[]{:S(2)}) %all-to-all-start.3) | async-done | bytes 8818464 | tf_op jit(solution)/shard_map/all_to_all | solution.py:245
  780.9 11.9 copy.207
  792.8 7.0 slice.233
  803.2 6.6 add_select_fusion
  809.8 22.4 %scatter-add.4 = f32[4,256,2128]{1,2,0:T(8,128)} dynamic-update-slice(f32[4,256,2128]{1,2,0:T(8,128)} %copy-done.8, f32[3,3,2128]{1,2,0:T(8,128)} %add_select_fusion, s32[]{:T(128)} %bitcast.52, s32[]{:T(128)} %bitcast.53, s32[]{:T(128)} %constant.140.clone.1) | dynamic-update-slice | bytes 153220 | tf_op jit(solution)/shard_map/scatter-add | solution.py:247
  838.1 6.5 copy.200
  844.6 15.7 %fusion.148 = f32[1024,2048]{1,0:T(8,128)} fusion(bf16[1024,2128]{1,0:T(8,128)(2,1)} %bitcast.319, bf16[2048,2128]{1,0:T(8,128)(2,1)} %concatenate.29), kind=kOutput, calls=%fused_computation.237 | convolution fusion | flops 8925478912 | bytes 21463040 | tf_op jit(solution)/shard_map/dot_general | solution.py:250
  864.7 50.2 %all_to_all.62 = bf16[256,4,1024]{0,2,1:T(8,128)(2,1)} all-to-all(bf16[256,4,1024]{0,2,1:T(8,128)(2,1)S(1)} %fusion.48), channel_id=1, replica_groups=mesh['dp'=8,'tp'=4] {'tp'}, dimensions={1} | all-to-all | bytes 4194304 | tf_op jit(solution)/shard_map/all_to_all | solution.py:193
  917.9 9.2 fusion.147
  927.1 9.1 convolution_bitcast_fusion
  936.2 12.9 fusion.149
  949.1 16.2 %pad_maximum_fusion = f32[2048,3152]{0,1:T(8,128)} fusion(f32[2048,1024]{0,1:T(8,128)} %convolution_bitcast_fusion, f32[2048,2128]{0,1:T(8,128)S(1)} %fusion.149), kind=kLoop, calls=%fused_computation.6 | loop fusion | flops 6455296 | bytes 51642368 | tf_op jit(solution)/shard_map/concatenate | solution.py:264
  972.4 13.2 all-reduce.17
  985.6 27.7 %all-reduce.16 = (f32[2048]{0:T(1024)}, f32[4352]{0:T(1024)}, f32[64]{0:T(128)}, f32[64]{0:T(128)}, f32[64]{0:T(128)}, /*index=5*/f32[4096]{0:T(1024)}) all-reduce(f32[2048]{0:T(1024)S(1)} %get-tuple-element.431, f32[4352]{0:T(1024)S(1)} %get-tuple-element.432, ...), channel_id=1, replica_groups=mesh['dp'=8,'tp'=4] {'dp'}, use_global_device_ids=true, to_apply=%region_31.32 | all-reduce | flops 10688 | bytes 85504 | tf_op jit(solution)/shard_map/psum | solution.py:283
  1013.4 47.0 %reduce-scatter.4.cloned.1.call-done = f32[256,2048]{1,0:T(8,128)} async-done(((f32[1024,2048]{1,0:T(8,128)}), f32[256,2048]{1,0:T(8,128)}) %reduce-scatter.4.cloned.1.call-update) | async-done | bytes 2097168 | tf_op jit(solution)/shard_map/reduce_scatter | solution.py:194
  1065.0 249.1 %reduce-scatter.8.cloned.1.call-done = f32[256,3152]{0,1:T(8,128)} async-done(((f32[2048,3152]{0,1:T(8,128)}), f32[256,3152]{0,1:T(8,128)}) %reduce-scatter.8.cloned.1.call-update) | async-done | bytes 3227664 | tf_op jit(solution)/shard_map/reduce_scatter | solution.py:263
  1322.5 44.8 %all-reduce.23.cloned.1.call-done = f32[4352,4]{0,1:T(4,128)} async-done(((f32[4352,4]{0,1:T(4,128)}), f32[4352,4]{0,1:T(4,128)}) %all-reduce.23.cloned.1.call-update) | async-done | bytes 69648 | tf_op jit(solution)/shard_map/psum | solution.py:283
  (273 shorter events, 199.5 us)
Async XLA Ops:
  7.2 59.1 %all-gather.8.cloned.1.call-start = ((), (), s32[]{:S(2)}) async-start(), calls=%async_computation.7 | async-start | bytes 5242880 | tf_op jit(solution)/shard_map/all_gather | solution.py:115
  106.0 8.6 copy-start.32
  106.0 72.0 %all-to-all-start = ((bf16[4,259,2128]{2,1,0:T(8,128)(2,1)}), bf16[4,259,2128]{2,1,0:T(8,128)(2,1)}, u32[]{:S(2)}, u32[]{:S(2)}) async-start(bf16[4,259,2128]{2,1,0:T(8,128)(2,1)} %pad_maximum_fusion.1), calls=%async_computation | async-start | bytes 9191424 | tf_op jit(solution)/shard_map/all_to_all | solution.py:120
  111.0 117.5 %all-gather.10.cloned.1.call-start = ((), (), s32[]{:S(2)}) async-start(), calls=%async_computation.9 | async-start | bytes 5242880 | tf_op jit(solution)/shard_map/all_gather | solution.py:201
  111.8 229.9 %all-gather.12.cloned.1.call-start = ((), (), s32[]{:S(2)}) async-start(), calls=%async_computation.14 | async-start | bytes 10485760 | tf_op jit(solution)/shard_map/all_gather | solution.py:12
  112.4 80.9 %copy-start.54 = (f32[64]{0:T(128)}, f32[64]{0:T(128)S(1)}, u32[]{:S(2)}) copy-start(f32[64]{0:T(128)S(1)} %exp.58) | copy-start | bytes 772
  116.2 105.2 %copy-start.49 = (pred[256]{0:T(512)(128)(4,1)}, pred[256]{0:T(512)(128)(4,1)S(1)}, u32[]{:S(2)}) copy-start(pred[256]{0:T(512)(128)(4,1)S(1)} %get-tuple-element.465) | copy-start | bytes 772
  116.2 419.6 %copy-start.40 = (f32[256]{0:T(256)}, f32[256]{0:T(256)S(1)}, u32[]{:S(2)}) copy-start(f32[256]{0:T(256)S(1)} %get-tuple-element.466) | copy-start | bytes 3076
  116.2 419.6 %copy-start.41 = (f32[256]{0:T(256)}, f32[256]{0:T(256)S(1)}, u32[]{:S(2)}) copy-start(f32[256]{0:T(256)S(1)} %get-tuple-element.467) | copy-start | bytes 3076
  116.2 419.6 %copy-start.42 = (f32[256]{0:T(256)}, f32[256]{0:T(256)S(1)}, u32[]{:S(2)}) copy-start(f32[256]{0:T(256)S(1)} %get-tuple-element.468) | copy-start | bytes 3076
  186.2 7.2 copy-start.45
  193.3 28.0 %copy-start.19 = (bf16[256,4,16]{0,2,1:T(8,128)(2,1)}, bf16[256,4,16]{0,2,1:T(8,128)(2,1)S(1)}, u32[]{:S(2)}) copy-start(bf16[256,4,16]{0,2,1:T(8,128)(2,1)S(1)} %slice.224) | copy-start | bytes 98308
  221.3 7.1 copy-start.47
  236.5 7.3 copy-start.24
  239.1 48.2 %all-to-all-start.2 = ((bf16[4,256,1024]{1,2,0:T(8,128)(2,1)}), bf16[4,256,1024]{1,2,0:T(8,128)(2,1)}, u32[]{:S(2)}, u32[]{:S(2)}) async-start(bf16[4,256,1024]{1,2,0:T(8,128)(2,1)} %copy.184), calls=%async_computation.3 | async-start | bytes 4194304 | tf_op jit(solution)/shard_map/all_to_all | solution.py:205
  243.7 238.2 %all-gather.14.cloned.1.call-start = ((), (), s32[]{:S(2)}) async-start(), calls=%async_computation.15 | async-start | bytes 10485760 | tf_op jit(solution)/shard_map/all_gather | solution.py:12
  298.8 55.9 %copy-start.21 = (f32[256,256]{1,0:T(8,128)}, f32[256,256]{1,0:T(8,128)S(1)}, u32[]{:S(2)}) copy-start(f32[256,256]{1,0:T(8,128)S(1)} %fusion.106) | copy-start | bytes 786436
  354.6 23.6 %copy-start.16 = (f32[256,64,64]{0,2,1:T(8,128)}, f32[256,64,64]{0,2,1:T(8,128)S(1)}, u32[]{:S(2)}) copy-start(f32[256,64,64]{0,2,1:T(8,128)S(1)} %fusion.100) | copy-start | bytes 12582916
  354.7 23.6 %copy-start.11 = (f32[4,256,1024]{1,2,0:T(8,128)S(1)}, f32[4,256,1024]{1,2,0:T(8,128)}, u32[]{:S(2)}) copy-start(f32[4,256,1024]{1,2,0:T(8,128)} %convert_element_type.132) | copy-start | bytes 12582916
  378.3 19.2 %copy-start.37 = (f32[256]{0:T(256)}, f32[256]{0:T(256)S(1)}, u32[]{:S(2)}) copy-start(f32[256]{0:T(256)S(1)} %fusion.132) | copy-start | bytes 3076
  414.6 8.8 copy-start.6
  423.4 6.7 copy-start.3
  423.4 6.7 copy-start.22
  496.8 9.9 copy-start.1
  496.8 9.9 copy-start.4
  553.8 7.3 copy-start.20
  553.9 7.3 copy-start.46
  553.9 7.3 copy-start.48
  553.9 7.3 copy-start.50
  553.9 7.6 copy-start.57
  553.9 7.6 copy-start.58
  553.9 7.8 copy-start.34
  553.9 7.8 copy-start.35
  553.9 10.7 copy-start.36
  553.9 10.6 copy-start.53
  554.0 10.6 copy-start.55
  631.5 7.2 copy-start.59
  631.5 7.9 copy-start.30
  631.5 149.4 %all-to-all-start.3 = ((f32[1,259,8512]{1,0,2:T(1,128)}), f32[1,259,8512]{1,0,2:T(1,128)}, u32[]{:S(2)}, u32[]{:S(2)}) async-start(f32[1,259,8512]{1,0,2:T(1,128)} %copy.197), calls=%async_computation.4 | async-start | bytes 26148864 | tf_op jit(solution)/shard_map/all_to_all | solution.py:245
  638.0 328.2 %all-reduce.21.cloned.1.call-start = ((), (), s32[]{:S(2)}) async-start(), calls=%async_computation.12 | async-start | bytes 139264 | tf_op jit(solution)/shard_map/psum | solution.py:284
  640.1 330.0 %reduce-scatter.6.cloned.1.call-start = ((), (), s32[]{:S(2)}) async-start(), calls=%async_computation.10 | async-start | bytes 10485760 | tf_op jit(solution)/shard_map/reduce_scatter | solution.py:249
  860.3 200.1 %reduce-scatter.4.cloned.1.call-start = ((), (), s32[]{:S(2)}) async-start(), calls=%async_computation.8 | async-start | bytes 10485760 | tf_op jit(solution)/shard_map/reduce_scatter | solution.py:194
  927.1 387.0 %reduce-scatter.8.cloned.1.call-start = ((), (), s32[]{:S(2)}) async-start(), calls=%async_computation.11 | async-start | bytes 29048832 | tf_op jit(solution)/shard_map/reduce_scatter | solution.py:263
  965.3 7.1 copy-start.52
  965.3 7.1 copy-start.29
  965.4 7.1 copy-start.56
  965.4 95.0 %copy-start.18 = (bf16[256,2048]{1,0:T(8,128)(2,1)S(1)}, bf16[256,2048]{1,0:T(8,128)(2,1)}, u32[]{:S(2)}) copy-start(bf16[256,2048]{1,0:T(8,128)(2,1)} %param.37) | copy-start | bytes 3145732
  965.4 401.9 %all-reduce.23.cloned.1.call-start = ((), (), s32[]{:S(2)}) async-start(), calls=%async_computation.13 | async-start | bytes 139264 | tf_op jit(solution)/shard_map/psum | solution.py:283
  (28 other events, 89.6 us)
Sparse Core Ops, SparseCore 0:
  11.5 54.7 all-gather.7
  113.7 83.3 all-gather.9
  228.6 113.0 all-gather.11
  394.2 87.6 all-gather.13
  642.0 162.0 all-reduce.20
  860.4 109.6 reduce-scatter.5
  973.2 87.1 reduce-scatter.3
  1062.9 251.2 reduce-scatter.7
  1316.5 50.8 all-reduce.22
